TPU v7x, 128 devices: a whole 4x4x4 slice. The times are simulated.
128 devices in a mesh: ep: 4 (over x), tm: 32 (over y, z, core).
Axes of the slice: x: 4, y: 4, z: 4, core: 2. Of those that a mesh axis runs over, the one named last changes fastest.
Arguments:
- predictions: float32 [128, 1048576], P('ep', 'tm'), may hold values from -6 to 6
- leaf_index: int32 [128, 1048576], P('ep', 'tm'), may hold values from 0 to 63
- events: int32 [128, 1048576], P('ep', 'tm'), may hold values 0 or 1
- tie_start: int32 [1048576], P('tm'), may hold values from 0 to 1, as said below
Outputs:
- new_pred: float32 [128, 1048576], P('ep', 'tm')
- leaf_weights: float32 [128, 64], P('ep')
- grad_hess: bfloat16 [2, 128, 32, 32768], P(None, None, 'tm', 'ep')
Inputs may be any that keep to these rules, and one draw needn't show every extreme that they name: `tie_start`: every row whose index is a multiple of 128 begins a tie group.
All inputs are finite; a program needn't handle non-finite values. No bound on the sum of `events` on one device may be relied on, other than what follows from the above.
Results may differ from a plain program's by a relative error of at most 0.0023.
Values may be sent and summed in bfloat16 or wider, within the bound.
A program may use at most 128 MiB of HBM per device.

v0:
```python
import math
import jax
import jax.numpy as jnp
from jax import lax
from jax.sharding import PartitionSpec as P

LEAVES = 64


def prefix(part, axis, combine, identity, reverse):
    count = lax.axis_size(axis)
    place = lax.axis_index(axis)
    ahead = count - 1 - place if reverse else place
    gathered = jax.tree.map(lambda a: lax.all_gather(a, axis), part)
    state = jax.tree.map(lambda a, e: jnp.zeros_like(a) + jnp.asarray(e, a.dtype), part, identity)

    def one(turn, state):
        source = count - 1 - turn if reverse else turn
        return combine(
            state, jax.tree.map(lambda a: lax.dynamic_index_in_dim(a, source, 0, False), gathered)
        )

    return lax.fori_loop(0, ahead, one, state)


def tile_matrices(tie_start):
    length = tie_start.shape[0]
    blocks = length // 128
    starts = tie_start.reshape(blocks, 128)
    labels = jnp.arange(128, dtype=jnp.int32)
    first_local = lax.cummax(jnp.where(starts == 1, labels[None, :], 0), axis=1)
    next_start = jnp.concatenate([starts[:, 1:], jnp.ones((blocks, 1), jnp.int32)], axis=1)
    last_local = lax.cummin(jnp.where(next_start == 1, labels[None, :], 127), axis=1, reverse=True)
    backward = (labels[None, :, None] >= first_local[:, None, :]).astype(jnp.float32)
    forward = (labels[None, :, None] <= last_local[:, None, :]).astype(jnp.float32)
    return (backward, forward)


def block_cumsum(values, matrices, from_end):
    groups = values.shape[0]
    length = values.shape[1]
    blocks = length // 128
    shaped = values.reshape(groups, blocks, 128)
    within = jnp.einsum("ebj,bji->ebi", shaped, matrices, precision=lax.Precision.HIGHEST)
    totals = jnp.sum(shaped, axis=2)
    if from_end:
        offsets = jnp.cumsum(totals[:, ::-1], axis=1)[:, ::-1] - totals
    else:
        offsets = jnp.cumsum(totals, axis=1) - totals
    return (within + offsets[:, :, None]).reshape(groups, length)


def add_values(earlier, later):
    return jax.tree.map(lambda left, right: left + right, earlier, later)


def leaf_partials(leaf_index, gradient, hessian, leaves):
    length = leaf_index.shape[1]
    width = math.gcd(length, 2048)
    labels = jnp.arange(leaves, dtype=jnp.int32)

    def one_block(step, totals):
        start = step * width
        part_leaf = lax.dynamic_slice_in_dim(leaf_index, start, width, 1)
        part_grad = lax.dynamic_slice_in_dim(gradient, start, width, 1)
        part_hess = lax.dynamic_slice_in_dim(hessian, start, width, 1)
        hits = part_leaf[:, None, :] == labels[None, :, None]
        gsum = jnp.sum(jnp.where(hits, part_grad[:, None, :], 0.0), axis=2)
        hsum = jnp.sum(jnp.where(hits, part_hess[:, None, :], 0.0), axis=2)
        return totals + jnp.stack([gsum, hsum], axis=1)

    empty = jnp.zeros((leaf_index.shape[0], 2, leaves), jnp.float32)
    return lax.fori_loop(0, length // width, one_block, empty)


def leaf_lookup(leaf_index, table):
    length = leaf_index.shape[1]
    width = math.gcd(length, 2048)
    labels = jnp.arange(table.shape[1], dtype=jnp.int32)

    def one_block(step, result):
        start = step * width
        part_leaf = lax.dynamic_slice_in_dim(leaf_index, start, width, 1)
        hits = part_leaf[:, None, :] == labels[None, :, None]
        picked = jnp.sum(jnp.where(hits, table[:, :, None], 0.0), axis=1)
        return lax.dynamic_update_slice_in_dim(result, picked, start, 1)

    empty = jnp.zeros(leaf_index.shape, jnp.float32)
    return lax.fori_loop(0, length // width, one_block, empty)


def on_device(predictions, leaf_index, events, tie_start):
    groups = predictions.shape[0]
    length = predictions.shape[1]
    backward, forward = tile_matrices(tie_start)
    weight = jnp.exp(predictions)
    local_risk = block_cumsum(weight, backward, True)
    block_total = local_risk[:, 0]
    zero_column = jnp.zeros((groups,), jnp.float32)
    later_total = prefix(block_total, "tm", add_values, zero_column, True)
    risk = local_risk + later_total[:, None]
    observed = events.astype(jnp.float32)
    inv_one = observed / risk
    inv_two = inv_one / risk
    local_one = block_cumsum(inv_one, forward, False)
    local_two = block_cumsum(inv_two, forward, False)
    totals_pair = (local_one[:, -1], local_two[:, -1])
    earlier_one, earlier_two = prefix(
        totals_pair, "tm", add_values, (zero_column, zero_column), False
    )
    accum_one = local_one + earlier_one[:, None]
    accum_two = local_two + earlier_two[:, None]
    gradient = weight * accum_one - observed
    hessian = weight * accum_one - weight * weight * accum_two
    stacked = jnp.stack([gradient, hessian]).astype(jnp.bfloat16).reshape(2, groups, 1, length)
    grad_hess = lax.all_to_all(stacked, "ep", split_axis=3, concat_axis=1, tiled=True)
    partial_value = leaf_partials(leaf_index, gradient, hessian, LEAVES)
    totals = lax.psum(partial_value, "tm")
    leaf_weights = -totals[:, 0] / (totals[:, 1] + 1.0)
    new_pred = predictions + leaf_lookup(leaf_index, leaf_weights)
    return (new_pred, leaf_weights, grad_hess)


def solution(mesh):
    placed = (P("ep", "tm"), P("ep", "tm"), P("ep", "tm"), P("tm"))
    return jax.shard_map(
        on_device,
        mesh=mesh,
        in_specs=placed,
        out_specs=(P("ep", "tm"), P("ep", None), P(None, None, "tm", "ep")),
        check_vma=False,
    )
```

profile of v0, /device:TPU:2, one launch (start us, length us, event | category | flops | bytes accessed | tf_op | source)
XLA Modules:
  0.0 666.5 jit_solution(1025747727024494581)
XLA Ops:
  0.6 6.2 exponential_bitcast_fusion.1
  12.6 10.0 %fusion.22 = f32[256,4,8,128]{3,2,1,0:T(8,128)S(1)} fusion(f32[4,256,8,128]{3,2,1,0:T(8,128)} %get-tuple-element.397, s32[256,128]{1,0:T(8,128)S(1)} %copy.130, f32[32,256]{0,1:T(8,128)S(1)} %copy.134), kind=kOutput, calls=%fused_computation.44 | convolution fusion | flops 1615855616 | bytes 8552448 | tf_op jit(solution)/shard_map/ebj,bji->ebi/dot_general | solution.py:44
  26.2 68.6 %all-reduce.1 = f32[1024]{0:T(1024)S(1)} all-reduce(f32[1024]{0:T(1024)S(1)} %dynamic-update-slice), channel_id=2, replica_groups=mesh['ep'=4,'tm'=32] {'tm'}, use_global_device_ids=true, to_apply=%add.1 | all-reduce | flops 1024 | bytes 8192
  101.0 9.3 %fusion.34 = (f32[4,8,256,128]{3,1,2,0:T(8,128)}, f32[4,256,8,128]{3,2,1,0:T(8,128)}, f32[4,256,8,128]{3,2,1,0:T(8,128)}, f32[4,8,256,128]{3,1,2,0:T(8,128)S(1)}) fusion(f32[32]{0:T(128)S(1)} %get-tuple-element.296, f32[256,4,8,128]{3,2,1,0:T(8,128)} %copy-done.1, s32[32,32768]{1,0:T(8,128)} %param.14), kind=kLoop, calls=%fused_computation.79 | loop fusion | flops 5242880 | bytes 25165952
  113.4 10.0 %fusion.21 = f32[256,4,8,128]{3,2,1,0:T(8,128)S(1)} fusion(f32[4,256,8,128]{3,2,1,0:T(8,128)} %get-tuple-element.394, s32[256,128]{1,0:T(8,128)S(1)} %copy.128, f32[32,256]{0,1:T(8,128)S(1)} %copy.139), kind=kOutput, calls=%fused_computation.42 | convolution fusion | flops 1615855616 | bytes 8552448 | tf_op jit(solution)/shard_map/ebj,bji->ebi/dot_general | solution.py:44
  130.0 10.0 %fusion.20 = f32[256,4,8,128]{3,2,1,0:T(8,128)S(1)} fusion(f32[4,256,8,128]{3,2,1,0:T(8,128)} %get-tuple-element.393, s32[256,128]{1,0:T(8,128)S(1)} %copy.128, f32[32,256]{0,1:T(8,128)S(1)} %copy.144), kind=kOutput, calls=%fused_computation.40 | convolution fusion | flops 1615855616 | bytes 8552448 | tf_op jit(solution)/shard_map/ebj,bji->ebi/dot_general | solution.py:44
  142.7 64.1 %all-reduce.4 = (f32[1024]{0:T(1024)S(1)}, f32[1024]{0:T(1024)S(1)}) all-reduce(f32[1024]{0:T(1024)S(1)} %dynamic-update-slice.1, f32[1024]{0:T(1024)S(1)} %dynamic-update-slice.2), channel_id=3, replica_groups=mesh['ep'=4,'tm'=32] {'tm'}, use_global_device_ids=true, to_apply=%add.2 | all-reduce | flops 2048 | bytes 16384
  206.9 10.2 %convert_bitcast_fusion = (bf16[1,32,1,32768]{3,1,2,0:T(8,128)(2,1)S(1)}, f32[32,32768]{1,0:T(8,128)}, bf16[1,32,1,32768]{3,1,2,0:T(8,128)(2,1)S(1)}, f32[32,32768]{1,0:T(8,128)}) fusion(f32[32]{0:T(128)S(1)} %get-tuple-element.298, f32[256,4,8,128]{3,2,1,0:T(8,128)} %copy-done.2, f32[32]{0:T(128)S(1)} %get-tuple-element.297, f32[256,4,8,128]{3,2,1,0:T(8,128)} %copy-done, ...), kind=kLoop, calls=%fused_computation.52 | loop fusion | flops 10485760 | bytes 29360384 | tf_op jit(solution)/shard_map/stack | solution.py:115
  219.5 33.0 %copy.146 = bf16[2,32,1,32768]{1,0,2,3:T(2,128)(2,1)} copy(bf16[2,32,1,32768]{3,1,2,0:T(8,128)(2,1)} %pad_maximum_fusion) | data formatting | bytes 8388608 | tf_op jit(solution)/shard_map/stack | solution.py:115
  252.5 19.2 %reshape.184 = bf16[4,2,262144]{2,1,0:T(2,128)(2,1)} reshape(bf16[32768,1,2,32]{3,2,1,0:T(2,128)(2,1)} %bitcast.143) | data formatting | bytes 8388608
  271.7 5.3 all-to-all-start
  277.1 117.7 %while.55 = (s32[]{:T(128)}, f32[32,2,64]{2,0,1:T(8,128)S(1)}, s32[32,32768]{1,0:T(8,128)}, f32[32,32768]{1,0:T(8,128)}, f32[32,32768]{1,0:T(8,128)}, /*index=5*/s32[]{:T(128)}, s32[]{:T(128)}, s32[]{:T(128)}, s32[]{:T(128)}) while((s32[]{:T(128)}, f32[32,2,64]{2,0,1:T(8,128)S(1)}, s32[32,32768]{1,0:T(8,128)}, ...), condition=%wide.region_18.19_spmd.clone, body=%wide.region_15.18_spmd.clone.sunk | while | flops 20979716 | bytes 2424997 | solution.py:73
  279.1 5.3 fusion.39
  286.5 5.3 fusion.39
  293.8 5.3 fusion.39
  301.2 5.3 fusion.39
  308.5 5.3 fusion.39
  315.9 5.3 fusion.39
  323.2 5.3 fusion.39
  330.6 5.3 fusion.39
  337.9 5.3 fusion.39
  345.3 5.3 fusion.39
  352.7 5.3 fusion.39
  360.0 5.3 fusion.39
  374.7 5.3 fusion.39
  382.1 5.3 fusion.39
  394.7 124.3 %psum.7 = f32[32,2,64]{2,0,1:T(8,128)S(1)} all-reduce(f32[32,2,64]{2,0,1:T(8,128)S(1)} %get-tuple-element.299), channel_id=1, replica_groups=mesh['ep'=4,'tm'=32] {'tm'}, use_global_device_ids=true, to_apply=%region_19.20 | all-reduce | flops 4096 | bytes 32768 | tf_op jit(solution)/shard_map/psum | solution.py:118
  521.3 80.5 %while.54 = (s32[]{:T(128)}, f32[32,32768]{1,0:T(8,128)}, s32[32,32768]{1,0:T(8,128)}, f32[32,64]{1,0:T(8,128)S(1)}, s32[]{:T(128)}, /*index=5*/s32[]{:T(128)}, s32[]{:T(128)}, s32[]{:T(128)}) while((s32[]{:T(128)}, f32[32,32768]{1,0:T(8,128)}, s32[32,32768]{1,0:T(8,128)}, f32[32,64]{1,0:T(8,128)S(1)}, s32[]{:T(128)}, ...), condition=%wide.region_22.23_spmd.clone, body=%wide.region_20.22_spmd.clone.sunk | while | flops 12517382 | bytes 1581203 | solution.py:89
  601.8 5.9 add.165
  607.7 12.0 %reshape.185 = bf16[32768,1,2,32]{3,2,1,0:T(2,128)(2,1)} reshape(bf16[4,2,262144]{2,1,0:T(2,128)(2,1)} %all-to-all-done) | data formatting | bytes 8388608
  619.7 40.0 %copy.150 = bf16[2,32,1,4,8192]{4,3,1,0,2:T(4,128)(2,1)} copy(bf16[2,32,1,4,8192]{1,0,4,3,2:T(2,128)(2,1)} %bitcast.144) | data formatting | bytes 8388608 | tf_op jit(solution)/shard_map/all_to_all | solution.py:116
  659.8 6.5 copy.148
  (208 shorter events, 156.1 us)
Async XLA Ops:
  0.6 6.2 copy-start.5
  22.6 2.0 copy-start.1
  22.6 2.1 copy-start.6
  123.4 2.1 copy-start
  123.4 3.7 copy-start.3
  140.0 2.0 copy-start.2
  271.7 336.0 %all-to-all-start = ((bf16[4,2,262144]{2,1,0:T(2,128)(2,1)}), bf16[4,2,262144]{2,1,0:T(2,128)(2,1)}, u32[]{:S(2)}, u32[]{:S(2)}) async-start(bf16[4,2,262144]{2,1,0:T(2,128)(2,1)} %reshape.184), calls=%async_computation | async-start | bytes 8388608 | tf_op jit(solution)/shard_map/all_to_all | solution.py:116
  601.8 5.9 copy-start.4
where the time goes:
time: 677 us; the launch traced here: 666 us
  blocking collectives  257 us (38%)
  local copies, waits for them, and re-layouts  195 us (29%)
  other arithmetic  176 us (26%)
  matrix products  30 us (4%)
    unnamed x2, blocking collectives  133 us
    psum x1, blocking collectives, on_device(): totals = lax.psum(partial_value, 'tm')  124 us
    reduce_sum x16, other arithmetic, one_block(): gsum = jnp.sum(jnp.where(hits, part_grad[:, None, :], 0.0), axis=2)  84.3 us
    reduce_sum x16, other arithmetic, one_block(): picked = jnp.sum(jnp.where(hits, table[:, :, None], 0.0), axis=1)  53.2 us
    unnamed x27, local copies, waits for them, and re-layouts  49.8 us
    all_to_all x2, local copies, waits for them, and re-layouts, on_device(): lax.all_to_all(stacked, 'ep', split_axis=3, concat_axis=1, tiled=True)  46.5 us
    another operation x1, local copies, waits for them, and re-layouts, on_device(): jnp.stack([gradient, hessian]).astype(jnp.bfloat16)  33 us
    dynamic_slice x32, local copies, waits for them, and re-layouts, one_block(): part_leaf = lax.dynamic_slice_in_dim(leaf_index, start, width, 1)  31.1 us
  transfers between devices with their start and end apart: 1, of which 0 were waited for; matrix products, arithmetic and copies ran while one was open for 31% of the time, Pallas kernels for 0%

commit v1 on v0

--- a/solution.py
+++ b/solution.py
@@ -115,7 +115,7 @@
     stacked = jnp.stack([gradient, hessian]).astype(jnp.bfloat16).reshape(2, groups, 1, length)
     grad_hess = lax.all_to_all(stacked, "ep", split_axis=3, concat_axis=1, tiled=True)
     partial_value = leaf_partials(leaf_index, gradient, hessian, LEAVES)
-    totals = lax.psum(partial_value, "tm")
+    totals = jnp.sum(lax.all_gather(partial_value, "tm"), axis=0)
     leaf_weights = -totals[:, 0] / (totals[:, 1] + 1.0)
     new_pred = predictions + leaf_lookup(leaf_index, leaf_weights)
     return (new_pred, leaf_weights, grad_hess)

time: 677 us -> 576 us (0.85)
  blocking collectives: 257 us -> 155 us
    psum x1 -> x0, blocking collectives: 124 us -> none  [on_device(): totals = lax.psum(partial_value, 'tm')]
    all_gather x0 -> x1, blocking collectives: none -> 22.1 us  [on_device(): totals = jnp.sum(lax.all_gather(partial_value, 'tm'), axis=0)]
  transfers between devices with their start and end apart: 1 -> 1, of which waited for: 0 -> 0; matrix products, arithmetic and copies ran while one was open for 31% -> 36% of each run, Pallas kernels for 0% -> 0%
where the time goes in v1:
time: 576 us; the launch traced here: 565 us
  local copies, waits for them, and re-layouts  195 us (34%)
  other arithmetic  177 us (31%)
  blocking collectives  155 us (27%)
  matrix products  30 us (5%)
    unnamed x2, blocking collectives  133 us
    reduce_sum x16, other arithmetic, one_block(): gsum = jnp.sum(jnp.where(hits, part_grad[:, None, :], 0.0), axis=2)  84.3 us
    reduce_sum x16, other arithmetic, one_block(): picked = jnp.sum(jnp.where(hits, table[:, :, None], 0.0), axis=1)  53.2 us
    unnamed x27, local copies, waits for them, and re-layouts  49.8 us
    all_to_all x2, local copies, waits for them, and re-layouts, on_device(): lax.all_to_all(stacked, 'ep', split_axis=3, concat_axis=1, tiled=True)  46.5 us
    another operation x1, local copies, waits for them, and re-layouts, on_device(): jnp.stack([gradient, hessian]).astype(jnp.bfloat16)  33 us
    dynamic_slice x32, local copies, waits for them, and re-layouts, one_block(): part_leaf = lax.dynamic_slice_in_dim(leaf_index, start, width, 1)  31.1 us
    dot_general x3, matrix products, block_cumsum(): jnp.einsum('ebj,bji->ebi', shaped, matrices, precision=lax.Precision.HIGH...  30 us
  transfers between devices with their start and end apart: 1, of which 0 were waited for; matrix products, arithmetic and copies ran while one was open for 36% of the time, Pallas kernels for 0%

profile of v1, /device:TPU:2, one launch (start us, length us, event | category | flops | bytes accessed | tf_op | source)
XLA Modules:
  0.0 564.8 jit_solution(10689830349634770257)
XLA Ops:
  0.6 6.2 %exponential_bitcast_fusion.1 = (f32[4,8,256,128]{3,1,2,0:T(8,128)}, f32[4,256,8,128]{3,2,1,0:T(8,128)}) fusion(f32[32,32768]{1,0:T(8,128)} %param.12), kind=kLoop, calls=%fused_computation.51 | loop fusion | bytes 12582912
  12.6 10.0 %fusion.22 = f32[256,4,8,128]{3,2,1,0:T(8,128)S(1)} fusion(f32[4,256,8,128]{3,2,1,0:T(8,128)} %get-tuple-element.397, s32[256,128]{1,0:T(8,128)S(1)} %copy.124, f32[32,256]{0,1:T(8,128)S(1)} %copy.128), kind=kOutput, calls=%fused_computation.44 | convolution fusion | flops 1615855616 | bytes 8552448 | tf_op jit(solution)/shard_map/ebj,bji->ebi/dot_general | solution.py:44
  26.2 68.6 %all-reduce.1 = f32[1024]{0:T(1024)S(1)} all-reduce(f32[1024]{0:T(1024)S(1)} %dynamic-update-slice), channel_id=2, replica_groups=mesh['ep'=4,'tm'=32] {'tm'}, use_global_device_ids=true, to_apply=%add.1 | all-reduce | flops 1024 | bytes 8192
  101.0 9.3 %fusion.33 = (f32[4,8,256,128]{3,1,2,0:T(8,128)}, f32[4,256,8,128]{3,2,1,0:T(8,128)}, f32[4,256,8,128]{3,2,1,0:T(8,128)}, f32[4,8,256,128]{3,1,2,0:T(8,128)S(1)}) fusion(f32[32]{0:T(128)S(1)} %get-tuple-element.296, f32[256,4,8,128]{3,2,1,0:T(8,128)} %copy-done.1, s32[32,32768]{1,0:T(8,128)} %param.14), kind=kLoop, calls=%fused_computation.78 | loop fusion | flops 5242880 | bytes 25165952
  113.4 10.0 %fusion.21 = f32[256,4,8,128]{3,2,1,0:T(8,128)S(1)} fusion(f32[4,256,8,128]{3,2,1,0:T(8,128)} %get-tuple-element.394, s32[256,128]{1,0:T(8,128)S(1)} %copy.122, f32[32,256]{0,1:T(8,128)S(1)} %copy.133), kind=kOutput, calls=%fused_computation.42 | convolution fusion | flops 1615855616 | bytes 8552448 | tf_op jit(solution)/shard_map/ebj,bji->ebi/dot_general | solution.py:44
  130.0 10.0 %fusion.20 = f32[256,4,8,128]{3,2,1,0:T(8,128)S(1)} fusion(f32[4,256,8,128]{3,2,1,0:T(8,128)} %get-tuple-element.393, s32[256,128]{1,0:T(8,128)S(1)} %copy.122, f32[32,256]{0,1:T(8,128)S(1)} %copy.138), kind=kOutput, calls=%fused_computation.40 | convolution fusion | flops 1615855616 | bytes 8552448 | tf_op jit(solution)/shard_map/ebj,bji->ebi/dot_general | solution.py:44
  142.7 64.1 %all-reduce.4 = (f32[1024]{0:T(1024)S(1)}, f32[1024]{0:T(1024)S(1)}) all-reduce(f32[1024]{0:T(1024)S(1)} %dynamic-update-slice.1, f32[1024]{0:T(1024)S(1)} %dynamic-update-slice.2), channel_id=3, replica_groups=mesh['ep'=4,'tm'=32] {'tm'}, use_global_device_ids=true, to_apply=%add.2 | all-reduce | flops 2048 | bytes 16384
  206.9 10.2 %convert_bitcast_fusion = (bf16[1,32,1,32768]{3,1,2,0:T(8,128)(2,1)S(1)}, f32[32,32768]{1,0:T(8,128)}, bf16[1,32,1,32768]{3,1,2,0:T(8,128)(2,1)S(1)}, f32[32,32768]{1,0:T(8,128)}) fusion(f32[32]{0:T(128)S(1)} %get-tuple-element.298, f32[256,4,8,128]{3,2,1,0:T(8,128)} %copy-done.2, f32[32]{0:T(128)S(1)} %get-tuple-element.297, f32[256,4,8,128]{3,2,1,0:T(8,128)} %copy-done, ...), kind=kLoop, calls=%fused_computation.52 | loop fusion | flops 10485760 | bytes 29360384 | tf_op jit(solution)/shard_map/stack | solution.py:115
  219.5 33.0 %copy.141 = bf16[2,32,1,32768]{1,0,2,3:T(2,128)(2,1)} copy(bf16[2,32,1,32768]{3,1,2,0:T(8,128)(2,1)} %pad_maximum_fusion) | data formatting | bytes 8388608 | tf_op jit(solution)/shard_map/stack | solution.py:115
  252.5 19.2 %reshape.185 = bf16[4,2,262144]{2,1,0:T(2,128)(2,1)} reshape(bf16[32768,1,2,32]{3,2,1,0:T(2,128)(2,1)} %bitcast.143) | data formatting | bytes 8388608
  271.7 5.3 all-to-all-start
  277.1 117.7 %while.55 = (s32[]{:T(128)}, f32[32,2,64]{2,0,1:T(8,128)S(1)}, s32[32,32768]{1,0:T(8,128)}, f32[32,32768]{1,0:T(8,128)}, f32[32,32768]{1,0:T(8,128)}, /*index=5*/s32[]{:T(128)}, s32[]{:T(128)}, s32[]{:T(128)}, s32[]{:T(128)}) while((s32[]{:T(128)}, f32[32,2,64]{2,0,1:T(8,128)S(1)}, s32[32,32768]{1,0:T(8,128)}, ...), condition=%wide.region_18.19_spmd.clone, body=%wide.region_15.18_spmd.clone.sunk | while | flops 20979716 | bytes 2424997 | solution.py:73
  279.1 5.3 fusion.38
  286.5 5.3 fusion.38
  293.8 5.3 fusion.38
  301.2 5.3 fusion.38
  308.5 5.3 fusion.38
  315.9 5.3 fusion.38
  323.2 5.3 fusion.38
  330.6 5.3 fusion.38
  337.9 5.3 fusion.38
  345.3 5.3 fusion.38
  352.7 5.3 fusion.38
  360.0 5.3 fusion.38
  374.7 5.3 fusion.38
  382.1 5.3 fusion.38
  394.7 22.1 %all-gather.3 = f32[1024,2,64]{2,1,0:T(2,128)S(1)} all-gather(f32[32,2,64]{2,1,0:T(2,128)S(1)} %copy.140), channel_id=5, replica_groups=mesh['ep'=4,'tm'=32] {'tm'}, dimensions={0}, use_global_device_ids=true | all-gather | bytes 540672 | tf_op jit(solution)/shard_map/all_gather | solution.py:118
  419.6 80.5 %while.54 = (s32[]{:T(128)}, f32[32,32768]{1,0:T(8,128)}, s32[32,32768]{1,0:T(8,128)}, f32[32,64]{1,0:T(8,128)S(1)}, s32[]{:T(128)}, /*index=5*/s32[]{:T(128)}, s32[]{:T(128)}, s32[]{:T(128)}) while((s32[]{:T(128)}, f32[32,32768]{1,0:T(8,128)}, s32[32,32768]{1,0:T(8,128)}, f32[32,64]{1,0:T(8,128)S(1)}, s32[]{:T(128)}, ...), condition=%wide.region_22.23_spmd.clone, body=%wide.region_20.22_spmd.clone.sunk | while | flops 12517382 | bytes 1581203 | solution.py:89
  500.1 5.9 %add.163 = f32[32,32768]{1,0:T(8,128)} add(f32[32,32768]{1,0:T(8,128)} %param.12, f32[32,32768]{1,0:T(8,128)} %get-tuple-element.300) | non-fusion elementwise | flops 1048576 | bytes 12582912 | tf_op jit(solution)/shard_map/add | solution.py:120
  506.0 12.0 %reshape.186 = bf16[32768,1,2,32]{3,2,1,0:T(2,128)(2,1)} reshape(bf16[4,2,262144]{2,1,0:T(2,128)(2,1)} %all-to-all-done) | data formatting | bytes 8388608
  518.0 40.0 %copy.145 = bf16[2,32,1,4,8192]{4,3,1,0,2:T(4,128)(2,1)} copy(bf16[2,32,1,4,8192]{1,0,4,3,2:T(2,128)(2,1)} %bitcast.144) | data formatting | bytes 8388608 | tf_op jit(solution)/shard_map/all_to_all | solution.py:116
  558.1 6.5 %copy.143 = bf16[2,4,32,1,8192]{4,2,1,0,3:T(8,128)(2,1)} copy(bf16[2,4,32,1,8192]{4,1,2,0,3:T(4,128)(2,1)} %bitcast.145) | data formatting | bytes 8388608 | tf_op jit(solution)/shard_map/all_to_all | solution.py:116
  (210 shorter events, 156.6 us)
Async XLA Ops:
  0.6 6.2 %copy-start.5 = (s32[32768]{0:T(1024)S(1)}, s32[32768]{0:T(1024)}, u32[]{:S(2)}) copy-start(s32[32768]{0:T(1024)} %param.15) | copy-start | bytes 393220
  22.6 2.0 copy-start.1
  22.6 2.1 copy-start.6
  123.4 2.1 copy-start
  123.4 3.7 copy-start.3
  140.0 2.0 copy-start.2
  271.7 234.3 %all-to-all-start = ((bf16[4,2,262144]{2,1,0:T(2,128)(2,1)}), bf16[4,2,262144]{2,1,0:T(2,128)(2,1)}, u32[]{:S(2)}, u32[]{:S(2)}) async-start(bf16[4,2,262144]{2,1,0:T(2,128)(2,1)} %reshape.185), calls=%async_computation | async-start | bytes 8388608 | tf_op jit(solution)/shard_map/all_to_all | solution.py:116
  500.1 5.9 %copy-start.4 = (f32[32,64]{1,0:T(8,128)}, f32[32,64]{1,0:T(8,128)S(1)}, u32[]{:S(2)}) copy-start(f32[32,64]{1,0:T(8,128)S(1)} %get-tuple-element.635) | copy-start | bytes 24580
